TPU v7x, 32 devices: a whole 2x2x4 slice. The times are simulated.
32 devices in a mesh: lat: 8 (over z, y), lon: 4 (over x, core).
Axes of the slice: x: 2, y: 2, z: 4, core: 2. Of those that a mesh axis runs over, the one named last changes fastest.
Arguments:
- pair_table: int32 [640], replicated, may hold values from 0 to 639, each once
- spectral: bfloat16 [640, 384, 1408], P('lat', 'lon'), may hold values from -0.071777344 to 0.071777344
- lat_basis: bfloat16 [640, 32, 1408], P('lat'), may hold values from -0.15625 to 0.15625
- in_weight: bfloat16 [192, 512], replicated, may hold values from -0.4375 to 0.4375
- in_bias: float32 [512], replicated, may hold values from -3 to 3
- out_weight: bfloat16 [512, 192], replicated, may hold values from -0.25 to 0.25
- out_bias: float32 [192], replicated, may hold values from -3 to 3
- cotangent: bfloat16 [64, 192, 2560], P('lat', None, 'lon'), may hold values from -0.08984375 to 0.08984375
Outputs:
- tendency: bfloat16 [64, 192, 2560], P('lat', None, 'lon')
- spectral_grad: bfloat16 [640, 384, 1408], P('lat', 'lon')
- in_weight_grad: float32 [192, 512], replicated
- in_bias_grad: float32 [512], replicated
- out_weight_grad: float32 [512, 192], replicated
- out_bias_grad: float32 [192], replicated
Inputs may be any that keep to these rules, and one draw needn't show every extreme that they name: `pair_table`: each pair number appears exactly once.
All inputs are finite; a program needn't handle non-finite values.
Results may differ from a plain program's by a relative error of at most 0.015.
Values may be sent and summed in bfloat16 or wider, within the bound.
No kernel may reach another device: no remote copies, remote signals or barrier semaphores. Data moves between devices by JAX's collectives and lax.ppermute only.
A program may use at most 256 MiB of HBM per device.

v0:
```python
import math

import jax
import jax.numpy as jnp
from jax import lax
from jax.sharding import PartitionSpec as P

TRUNC = 1279


def pair_masks(pair_ids, length):
    first_len = TRUNC + 1 - pair_ids
    position = jnp.arange(length, dtype=jnp.int32)[None, :]
    lower_part = position < first_len[:, None]
    upper_part = jnp.logical_and(position >= first_len[:, None], position < TRUNC + 2)
    offset = jnp.where(lower_part, position, position - first_len[:, None])
    parity = jnp.where(offset % 2 == 0, 1.0, -1.0).astype(jnp.float32)
    return (lower_part, upper_part, parity, first_len)


def wave_numbers(pair_ids):
    both = jnp.stack([pair_ids, TRUNC - pair_ids], axis=1)
    return both.reshape(-1)


def fourier_table(numbers, longitudes, lon_total):
    phase = numbers[:, None] * longitudes[None, :] % lon_total
    angle = phase.astype(jnp.float32) * (2.0 * math.pi / lon_total)
    factor = jnp.where(numbers == 0, 1.0, 2.0).astype(jnp.float32)[:, None]
    return jnp.stack([factor * jnp.cos(angle), -factor * jnp.sin(angle)], axis=1).astype(
        jnp.bfloat16
    )


def split_parts(coeffs, lower_part, upper_part):
    empty = jnp.zeros_like(coeffs)
    return jnp.stack(
        [
            jnp.where(lower_part[:, None, :], coeffs, empty),
            jnp.where(upper_part[:, None, :], coeffs, empty),
        ],
        axis=1,
    )


def per_device(
    pair_table, spectral, lat_basis, in_weight, in_bias, out_weight, out_bias, cotangent
):
    pair_dev = spectral.shape[0]
    width_local = spectral.shape[1]
    band_rows = cotangent.shape[0]
    block_cols = cotangent.shape[2]
    lon_total = block_cols * lax.axis_size("lon")
    first_row = lax.axis_index("lat") * pair_dev
    local_ids = lax.dynamic_slice_in_dim(pair_table, first_row, pair_dev)
    lower_part, upper_part, parity, first_len = pair_masks(local_ids, spectral.shape[2])
    mirrored = jnp.flip(lat_basis * parity[:, None, :].astype(jnp.bfloat16), axis=1)
    full_basis = jnp.concatenate([lat_basis, mirrored], axis=1)
    lat_window = full_basis.shape[1]
    masked = split_parts(spectral, lower_part, upper_part)
    waves = jnp.einsum(
        "pqkj,plj->pqlk", masked, full_basis, preferred_element_type=jnp.float32
    ).astype(jnp.bfloat16)
    flat_waves = waves.reshape(2 * pair_dev, lat_window * width_local)
    band_waves = lax.all_to_all(flat_waves, "lat", split_axis=1, concat_axis=0, tiled=True)
    wave_count = band_waves.shape[0]
    coeff_grid = band_waves.reshape(wave_count, band_rows, width_local // 2, 2)
    numbers = wave_numbers(pair_table)
    full_table = fourier_table(numbers, jnp.arange(lon_total, dtype=jnp.int32), lon_total)
    all_columns = jnp.einsum(
        "glkc,gcn->lkn", coeff_grid, full_table, preferred_element_type=jnp.float32
    ).astype(jnp.bfloat16)
    grid = lax.all_to_all(all_columns, "lon", split_axis=2, concat_axis=1, tiled=True)
    pre_act = (
        jnp.einsum("lkc,kh->lch", grid, in_weight, preferred_element_type=jnp.float32) + in_bias
    )
    activated, gelu_back = jax.vjp(jax.nn.gelu, pre_act)
    hidden = activated.astype(jnp.bfloat16)
    tendency = (
        jnp.einsum("lch,hk->lkc", hidden, out_weight, preferred_element_type=jnp.float32)
        + out_bias[None, :, None]
    ).astype(jnp.bfloat16)
    out_weight_part = jnp.einsum(
        "lch,lkc->hk", hidden, cotangent, preferred_element_type=jnp.float32
    )
    out_bias_part = jnp.sum(cotangent.astype(jnp.float32), axis=(0, 2))
    hidden_grad = jnp.einsum(
        "lkc,hk->lch", cotangent, out_weight, preferred_element_type=jnp.float32
    )
    pre_grad = gelu_back(hidden_grad)[0].astype(jnp.bfloat16)
    in_weight_part = jnp.einsum("lkc,lch->kh", grid, pre_grad, preferred_element_type=jnp.float32)
    in_bias_part = jnp.sum(pre_grad.astype(jnp.float32), axis=(0, 1))
    grid_grad = jnp.einsum(
        "lch,kh->lkc", pre_grad, in_weight, preferred_element_type=jnp.float32
    ).astype(jnp.bfloat16)
    in_weight_grad, in_bias_grad, out_weight_grad, out_bias_grad = lax.psum(
        (in_weight_part, in_bias_part, out_weight_part, out_bias_part), ("lat", "lon")
    )
    level_rows = lax.all_to_all(grid_grad, "lon", split_axis=1, concat_axis=2, tiled=True)
    wave_grad = jnp.einsum(
        "gcn,lkn->glkc", full_table, level_rows, preferred_element_type=jnp.float32
    ).astype(jnp.bfloat16)
    flat_grad = wave_grad.reshape(wave_count, band_rows * width_local)
    pair_grad = lax.all_to_all(flat_grad, "lat", split_axis=0, concat_axis=1, tiled=True)
    pair_grad = pair_grad.reshape(pair_dev, 2, lat_window, width_local)
    contrib = jnp.einsum(
        "pqlk,plj->pqkj", pair_grad, full_basis, preferred_element_type=jnp.float32
    )
    empty = jnp.zeros_like(contrib[:, 0])
    spectral_grad = (
        jnp.where(lower_part[:, None, :], contrib[:, 0], empty)
        + jnp.where(upper_part[:, None, :], contrib[:, 1], empty)
    ).astype(jnp.bfloat16)
    return (tendency, spectral_grad, in_weight_grad, in_bias_grad, out_weight_grad, out_bias_grad)


def solution(mesh):
    placed = (
        P(),
        P("lat", "lon", None),
        P("lat", None, None),
        P(),
        P(),
        P(),
        P(),
        P("lat", None, "lon"),
    )
    return jax.shard_map(
        per_device,
        mesh=mesh,
        in_specs=placed,
        out_specs=(P("lat", None, "lon"), P("lat", "lon", None), P(), P(), P(), P()),
        check_vma=False,
    )
```

profile of v0, /device:TPU:0, one launch (start us, length us, event | category | flops | bytes accessed | tf_op | source)
XLA Modules:
  0.0 471.3 jit_solution(12344877415564866981)
XLA Ops:
  8.6 7.0 %broadcast_multiply_fusion = bf16[80,32,1408]{2,1,0:T(8,128)(2,1)} fusion(bf16[80,32,1408]{2,1,0:T(8,128)(2,1)} %param.10, bf16[80,1408]{1,0:T(8,128)(2,1)S(1)} %select_convert_fusion), kind=kLoop, calls=%fused_computation.43 | loop fusion | flops 3604480 | bytes 14643200 | tf_op jit(solution)/shard_map/mul | solution.py:57
  15.6 20.3 %rev.4 = bf16[80,32,1408]{2,1,0:T(8,128)(2,1)} reverse(bf16[80,32,1408]{2,1,0:T(8,128)(2,1)} %broadcast_multiply_fusion), dimensions={1} | reverse | bytes 14417920 | tf_op jit(solution)/shard_map/jit(_flip)/rev | solution.py:57
  35.9 23.5 %select_bitcast_fusion.1 = (bf16[80,1,96,1408]{3,2,1,0:T(8,128)(2,1)}, bf16[80,1,96,1408]{3,2,1,0:T(8,128)(2,1)}) fusion(bf16[80,96,1408]{2,1,0:T(8,128)(2,1)} %param.9, pred[80,1408]{1,0:T(8,128)(4,1)S(1)} %get-tuple-element.16, pred[80,1408]{1,0:T(8,128)(4,1)S(1)} %get-tuple-element.17), kind=kLoop, calls=%fused_computation.11 | loop fusion | flops 21626880 | bytes 65105920 | tf_op jit(solution)/shard_map/stack | solution.py:37
  59.4 24.7 %convert_bitcast_fusion = bf16[80,2,64,96]{3,2,1,0:T(8,128)(2,1)} fusion(bf16[80,1,96,1408]{3,2,1,0:T(8,128)(2,1)} %get-tuple-element.11, bf16[80,1,96,1408]{3,2,1,0:T(8,128)(2,1)} %get-tuple-element.10, bf16[80,32,1408]{2,1,0:T(8,128)(2,1)} %rev.4, bf16[80,32,1408]{2,1,0:T(8,128)(2,1)} %param.10), kind=kOutput, calls=%fused_computation.47 | convolution fusion | flops 2884567040 | bytes 59637760 | tf_op jit(solution)/shard_map/pqkj,plj->pqlk/dot_general | solution.py:61
  90.1 7.8 %all-to-all-start = ((bf16[160,8,768]{2,0,1:T(8,128)(2,1)}), bf16[160,8,768]{2,0,1:T(8,128)(2,1)S(1)}, u32[]{:S(2)}, u32[]{:S(2)}) async-start(bf16[160,8,768]{2,0,1:T(8,128)(2,1)} %copy.30), calls=%async_computation | async-start | bytes 3932160 | tf_op jit(solution)/shard_map/all_to_all | solution.py:65
  98.4 58.1 %multiply_convert_fusion.1 = (bf16[1280,1,2560]{2,0,1:T(8,128)(2,1)}, bf16[1280,1,2560]{2,0,1:T(8,128)(2,1)}) fusion(s32[1280]{0:T(1024)S(1)} %reshape.286, f32[1280]{0:T(1024)S(1)} %get-tuple-element.14, f32[1280]{0:T(1024)S(1)} %get-tuple-element.15), kind=kLoop, calls=%fused_computation.23 | loop fusion | flops 42598400 | bytes 13122560 | tf_op jit(solution)/shard_map/convert
  161.9 5.2 %reshape.285 = bf16[1280,8,48,2]{0,3,2,1:T(2,128)(2,1)} reshape(bf16[8,160,768]{1,0,2:T(8,128)(2,1)S(1)} %copy.31) | data formatting | bytes 3932160 | tf_op jit(solution)/shard_map/reshape | solution.py:67
  167.1 9.0 %fusion.26 = bf16[8,48,2560]{2,1,0:T(8,128)(2,1)S(1)} fusion(bf16[1280,1,2560]{2,0,1:T(8,128)(2,1)} %get-tuple-element.13, bf16[1280,1,2560]{2,0,1:T(8,128)(2,1)} %get-tuple-element.12, bf16[1280,8,48,2]{0,3,2,1:T(2,128)(2,1)} %reshape.285), kind=kOutput, calls=%fused_computation.40 | convolution fusion | flops 5040701440 | bytes 17039360 | tf_op jit(solution)/shard_map/glkc,gcn->lkn/dot_general | solution.py:70
  176.1 5.2 %copy.34 = bf16[8,48,2560]{1,0,2:T(8,128)(2,1)} copy(bf16[8,48,2560]{2,1,0:T(8,128)(2,1)S(1)} %fusion.26) | data formatting | bytes 3932160 | tf_op jit(solution)/shard_map/convert_element_type | solution.py:72
  181.3 8.8 %reshape.297 = bf16[4,2,122880]{2,1,0:T(2,128)(2,1)S(1)} reshape(bf16[2560,8,48]{2,1,0:T(8,128)(2,1)} %bitcast.101) | data formatting | bytes 3932160
  190.2 27.7 %all_to_all.68 = bf16[4,2,122880]{2,1,0:T(2,128)(2,1)} all-to-all(bf16[4,2,122880]{2,1,0:T(2,128)(2,1)S(1)} %reshape.297), channel_id=1, replica_groups=mesh['lat'=8,'lon'=4] {'lon'}, dimensions={0} | all-to-all | bytes 3932160 | tf_op jit(solution)/shard_map/all_to_all | solution.py:73
  217.9 7.0 %reshape.298 = bf16[2560,8,48]{2,1,0:T(8,128)(2,1)} reshape(bf16[4,2,122880]{2,1,0:T(2,128)(2,1)} %all_to_all.68) | data formatting | bytes 3932160
  224.9 5.7 %copy.35 = bf16[8,48,4,640]{3,1,2,0:T(8,128)(2,1)S(1)} copy(bf16[8,48,4,640]{1,0,3,2:T(8,128)(2,1)} %bitcast.102) | data formatting | bytes 3932160 | tf_op jit(solution)/shard_map/all_to_all | solution.py:73
  230.7 5.5 %multiply_convert_fusion.2 = (bf16[8,640,512]{2,1,0:T(8,128)(2,1)}, f32[8,640,512]{2,1,0:T(8,128)S(1)}) fusion(f32[512]{0:T(512)S(1)} %copy-done.13, bf16[8,192,640]{2,1,0:T(8,128)(2,1)S(1)} %bitcast.107, bf16[192,512]{1,0:T(8,128)(2,1)S(1)} %copy-done), kind=kOutput, calls=%fused_computation.36 | convolution fusion | flops 1032847360 | bytes 17893376 | tf_op jit(solution)/shard_map/lkc,kh->lch/dot_general | solution.py:75
  236.2 8.7 %convert_reduce_fusion = (f32[512]{0:T(512)S(1)}, bf16[8,640,512]{2,1,0:T(8,128)(2,1)S(1)}) fusion(f32[8,640,512]{2,1,0:T(8,128)S(1)} %get-tuple-element.19, f32[512]{0:T(512)S(1)} %copy-done.13, bf16[8,192,640]{2,1,0:T(8,128)(2,1)S(1)} %copy-done.4, bf16[512,192]{0,1:T(8,128)(2,1)S(1)} %copy-done.12), kind=kOutput, calls=%fused_computation.35 | convolution fusion | flops 1066925568 | bytes 17895424 | tf_op jit(solution)/shard_map/lkc,hk->lch/dot_general | solution.py:87
  247.9 27.0 %all_to_all.69 = bf16[8,192,640]{2,0,1:T(8,128)(2,1)S(1)} all-to-all(bf16[8,192,640]{2,0,1:T(8,128)(2,1)S(1)} %copy.36), channel_id=1, replica_groups=mesh['lat'=8,'lon'=4] {'lon'}, dimensions={1} | all-to-all | bytes 3932160 | tf_op jit(solution)/shard_map/all_to_all | solution.py:99
  278.6 9.0 %fusion.28 = bf16[1280,8,48,2]{0,2,3,1:T(8,128)(2,1)S(1)} fusion(bf16[1280,1,2560]{2,0,1:T(8,128)(2,1)} %get-tuple-element.13, bf16[1280,1,2560]{2,0,1:T(8,128)(2,1)} %get-tuple-element.12, bf16[8,48,2560,1]{2,1,0,3:T(8,128)(2,1)} %reshape.293), kind=kOutput, calls=%fused_computation.45 | convolution fusion | flops 5060362240 | bytes 17039360 | tf_op jit(solution)/shard_map/gcn,lkn->glkc/dot_general | solution.py:100
  290.3 6.4 %all_to_all.61 = bf16[8,160,768]{1,0,2:T(8,128)(2,1)S(1)} reshape(bf16[1280,8,48,2]{0,3,2,1:T(2,128)(2,1)} %copy.38) | data formatting | bytes 3932160 | tf_op jit(solution)/shard_map/all_to_all | solution.py:104
  300.0 6.0 %all-to-all-start.3 = ((bf16[8,160,768]{2,1,0:T(8,128)(2,1)}), bf16[8,160,768]{2,1,0:T(8,128)(2,1)S(1)}, u32[]{:S(2)}, u32[]{:S(2)}) async-start(bf16[8,160,768]{2,1,0:T(8,128)(2,1)} %copy.39), calls=%async_computation.3 | async-start | bytes 3932160 | tf_op jit(solution)/shard_map/all_to_all | solution.py:104
  308.1 5.0 %convolution_bitcast_fusion.1 = f32[192,512]{1,0:T(8,128)} fusion(bf16[8,192,640]{2,1,0:T(8,128)(2,1)} %bitcast.108, bf16[8,640,512]{2,1,0:T(8,128)(2,1)} %copy-done.3), kind=kOutput, calls=%fused_computation.54 | convolution fusion | flops 1006632960 | bytes 7602176 | tf_op jit(solution)/shard_map/lkc,lch->kh/dot_general | solution.py:91
  317.6 56.6 %all-reduce = (f32[512]{0:T(512)}, f32[192]{0:T(256)}) all-reduce(f32[512]{0:T(512)S(1)} %get-tuple-element.20, f32[192]{0:T(256)S(1)} %convert_reduce_fusion.1), channel_id=1, replica_groups=mesh['lat'=8,'lon'=4] {'lat','lon'}, use_global_device_ids=true, to_apply=%region_2.3 | all-reduce | flops 704 | bytes 5632 | tf_op jit(solution)/shard_map/psum | solution.py:96
  374.3 5.6 %fusion.36 = bf16[8,192,640]{2,1,0:T(8,128)(2,1)} fusion(f32[192]{0:T(256)S(1)} %copy-done.14, bf16[8,640,512]{2,1,0:T(8,128)(2,1)} %get-tuple-element.18, bf16[512,192]{0,1:T(8,128)(2,1)S(1)} %copy-done.12), kind=kOutput, calls=%fused_computation.52 | convolution fusion | flops 1008599040 | bytes 7406336 | tf_op jit(solution)/shard_map/lch,hk->lkc/dot_general | solution.py:80
  386.8 34.6 %fusion.9 = f32[80,2,96,1408]{3,2,0,1:T(8,128)} fusion(bf16[80,32,1408]{2,1,0:T(8,128)(2,1)} %rev.4, bf16[80,32,1408]{2,1,0:T(8,128)(2,1)} %param.10, bf16[80,2,64,96]{3,2,1,0:T(8,128)(2,1)S(1)} %reshape.287), kind=kOutput, calls=%fused_computation.17 | convolution fusion | flops 2797076480 | bytes 102891520 | tf_op jit(solution)/shard_map/pqlk,plj->pqkj/dot_general | solution.py:106
  421.5 36.2 %fusion.2 = bf16[80,96,1408]{2,1,0:T(8,128)(2,1)} fusion(f32[80,2,96,1408]{3,2,0,1:T(8,128)} %fusion.9, pred[80,1408]{1,0:T(8,128)(4,1)S(1)} %copy-done.10, pred[80,1408]{1,0:T(8,128)(4,1)S(1)} %copy-done.8), kind=kLoop, calls=%fused_computation.3 | loop fusion | flops 43253760 | bytes 108359680 | tf_op jit(solution)/shard_map/convert_element_type | solution.py:113
  (61 shorter events, 45.8 us)
Async XLA Ops:
  7.2 223.5 %copy-start = (bf16[192,512]{1,0:T(8,128)(2,1)S(1)}, bf16[192,512]{1,0:T(8,128)(2,1)}, u32[]{:S(2)}) copy-start(bf16[192,512]{1,0:T(8,128)(2,1)} %param.11) | copy-start | bytes 589828
  8.6 27.4 %copy-start.7 = (pred[80,1408]{1,0:T(8,128)(4,1)}, pred[80,1408]{1,0:T(8,128)(4,1)S(1)}, u32[]{:S(2)}) copy-start(pred[80,1408]{1,0:T(8,128)(4,1)S(1)} %get-tuple-element.16) | copy-start | bytes 337924
  8.6 27.4 %copy-start.9 = (pred[80,1408]{1,0:T(8,128)(4,1)}, pred[80,1408]{1,0:T(8,128)(4,1)S(1)}, u32[]{:S(2)}) copy-start(pred[80,1408]{1,0:T(8,128)(4,1)S(1)} %get-tuple-element.17) | copy-start | bytes 337924
  84.1 13.9 %copy-start.11 = (s32[640]{0:T(1024)S(1)}, s32[640]{0:T(1024)}, u32[]{:S(2)}) copy-start(s32[640]{0:T(1024)} %param.8) | copy-start | bytes 7684
  90.1 66.4 %all-to-all-start = ((bf16[160,8,768]{2,0,1:T(8,128)(2,1)}), bf16[160,8,768]{2,0,1:T(8,128)(2,1)S(1)}, u32[]{:S(2)}, u32[]{:S(2)}) async-start(bf16[160,8,768]{2,0,1:T(8,128)(2,1)} %copy.30), calls=%async_computation | async-start | bytes 3932160 | tf_op jit(solution)/shard_map/all_to_all | solution.py:65
  156.5 1.3 copy-start.2
  190.2 40.5 %copy-start.13 = (f32[512]{0:T(512)S(1)}, f32[512]{0:T(512)}, u32[]{:S(2)}) copy-start(f32[512]{0:T(512)} %param.12) | copy-start | bytes 6148
  230.7 5.6 %copy-start.6 = (bf16[8,48,4,640]{3,1,2,0:T(8,128)(2,1)}, bf16[8,48,4,640]{3,1,2,0:T(8,128)(2,1)S(1)}, u32[]{:S(2)}) copy-start(bf16[8,48,4,640]{3,1,2,0:T(8,128)(2,1)S(1)} %copy.35) | copy-start | bytes 5898244
  230.7 5.5 %copy-start.4 = (bf16[8,192,640]{2,1,0:T(8,128)(2,1)S(1)}, bf16[8,192,640]{2,1,0:T(8,128)(2,1)}, u32[]{:S(2)}) copy-start(bf16[8,192,640]{2,1,0:T(8,128)(2,1)} %param.15) | copy-start | bytes 5898244
  230.7 5.5 %copy-start.12 = (bf16[512,192]{0,1:T(8,128)(2,1)S(1)}, bf16[512,192]{0,1:T(8,128)(2,1)}, u32[]{:S(2)}) copy-start(bf16[512,192]{0,1:T(8,128)(2,1)} %param.13) | copy-start | bytes 589828
  244.9 31.5 %copy-start.3 = (bf16[8,640,512]{2,1,0:T(8,128)(2,1)}, bf16[8,640,512]{2,1,0:T(8,128)(2,1)S(1)}, u32[]{:S(2)}) copy-start(bf16[8,640,512]{2,1,0:T(8,128)(2,1)S(1)} %get-tuple-element.21) | copy-start | bytes 15728644
  300.0 79.9 %all-to-all-start.3 = ((bf16[8,160,768]{2,1,0:T(8,128)(2,1)}), bf16[8,160,768]{2,1,0:T(8,128)(2,1)S(1)}, u32[]{:S(2)}, u32[]{:S(2)}) async-start(bf16[8,160,768]{2,1,0:T(8,128)(2,1)} %copy.39), calls=%async_computation.3 | async-start | bytes 3932160 | tf_op jit(solution)/shard_map/all_to_all | solution.py:104
  306.0 154.6 %all-reduce.4.cloned.1.call-start = ((), (), s32[]{:S(2)}) async-start(), calls=%async_computation.4 | async-start | bytes 1572864 | tf_op jit(solution)/shard_map/psum | solution.py:96
  306.1 7.1 %copy-start.5 = (bf16[8,192,640]{2,1,0:T(8,128)(2,1)S(1)}, bf16[8,192,640]{2,1,0:T(8,128)(2,1)}, u32[]{:S(2)}) copy-start(bf16[8,192,640]{2,1,0:T(8,128)(2,1)} %param.15) | copy-start | bytes 5898244
  308.1 66.1 %copy-start.14 = (f32[192]{0:T(256)S(1)}, f32[192]{0:T(256)}, u32[]{:S(2)}) copy-start(f32[192]{0:T(256)} %param.14) | copy-start | bytes 2308
  386.8 34.6 %copy-start.8 = (pred[80,1408]{1,0:T(8,128)(4,1)S(1)}, pred[80,1408]{1,0:T(8,128)(4,1)}, u32[]{:S(2)}) copy-start(pred[80,1408]{1,0:T(8,128)(4,1)} %copy-done.7) | copy-start | bytes 337924
  386.8 34.6 %copy-start.10 = (pred[80,1408]{1,0:T(8,128)(4,1)S(1)}, pred[80,1408]{1,0:T(8,128)(4,1)}, u32[]{:S(2)}) copy-start(pred[80,1408]{1,0:T(8,128)(4,1)} %copy-done.9) | copy-start | bytes 337924
  421.4 42.7 %copy-start.1 = (bf16[192,512]{1,0:T(8,128)(2,1)S(1)}, bf16[192,512]{1,0:T(8,128)(2,1)}, u32[]{:S(2)}) copy-start(bf16[192,512]{1,0:T(8,128)(2,1)} %param.11) | copy-start | bytes 589828
Sparse Core Ops, SparseCore 0:
  317.7 142.8 all-reduce.3
where the time goes:
time: 477 us; the launch traced here: 471 us
  other arithmetic  128 us (27%)
  blocking collectives  111 us (23%)
  matrix products  108 us (23%)
  local copies, waits for them, and re-layouts  91.9 us (19%)
  between operations  14.6 us (3%)
  starting transfers between devices  13.9 us (3%)
    another operation x1, other arithmetic  58.1 us
    psum x1, blocking collectives, per_device(): lax.psum((in_weight_part, in_bias_part, out_weight_part, out_bias_part),...  56.6 us
    convert_element_type x1, other arithmetic, per_device(): spectral_grad = (jnp.where(lower_part[:, None, :], contrib[:, 0], empty)...  36.2 us
    dot_general x1, matrix products, per_device(): jnp.einsum('pqlk,plj->pqkj', pair_grad, full_basis, preferred_element_typ...  34.6 us
    all_to_all x1, blocking collectives, per_device(): lax.all_to_all(all_columns, 'lon', split_axis=2, concat_axis=1, tiled=True)  27.7 us
    all_to_all x1, blocking collectives, per_device(): lax.all_to_all(grid_grad, 'lon', split_axis=1, concat_axis=2, tiled=True)  27 us
    dot_general x1, matrix products, per_device(): jnp.einsum('pqkj,plj->pqlk', masked, full_basis, preferred_element_type=j...  24.7 us
    another operation x1, other arithmetic, split_parts(): jnp.stack([jnp.where(lower_part[:, None, :], coeffs, empty), jnp.where(up...  23.5 us
  transfers between devices with their start and end apart: 3, of which 1 were waited for; matrix products, arithmetic and copies ran while one was open for 33% of the time, Pallas kernels for 0%

commit v1 on v0

--- a/solution.py
+++ b/solution.py
@@ -23,24 +23,27 @@
     return both.reshape(-1)
 
 
-def fourier_table(numbers, longitudes, lon_total):
-    phase = numbers[:, None] * longitudes[None, :] % lon_total
-    angle = phase.astype(jnp.float32) * (2.0 * math.pi / lon_total)
+def fourier_table(numbers, lon_total):
+    step = 128 if lon_total % 128 == 0 else 1
+    coarse = jnp.arange(lon_total // step, dtype=jnp.int32) * step
+    fine = jnp.arange(step, dtype=jnp.int32)
+    scale = 2.0 * math.pi / lon_total
+
+    def angles(offsets):
+        phase = numbers[:, None] * offsets[None, :] % lon_total
+        angle = phase.astype(jnp.float32) * scale
+        return jnp.cos(angle), jnp.sin(angle)
+
+    cos_a, sin_a = angles(coarse)
+    cos_b, sin_b = angles(fine)
+    cos_t = cos_a[:, :, None] * cos_b[:, None, :] - sin_a[:, :, None] * sin_b[:, None, :]
+    sin_t = sin_a[:, :, None] * cos_b[:, None, :] + cos_a[:, :, None] * sin_b[:, None, :]
+    count = numbers.shape[0]
     factor = jnp.where(numbers == 0, 1.0, 2.0).astype(jnp.float32)[:, None]
-    return jnp.stack([factor * jnp.cos(angle), -factor * jnp.sin(angle)], axis=1).astype(
-        jnp.bfloat16
-    )
-
-
-def split_parts(coeffs, lower_part, upper_part):
-    empty = jnp.zeros_like(coeffs)
     return jnp.stack(
-        [
-            jnp.where(lower_part[:, None, :], coeffs, empty),
-            jnp.where(upper_part[:, None, :], coeffs, empty),
-        ],
+        [factor * cos_t.reshape(count, lon_total), -factor * sin_t.reshape(count, lon_total)],
         axis=1,
-    )
+    ).astype(jnp.bfloat16)
 
 
 def per_device(
@@ -48,25 +51,37 @@
 ):
     pair_dev = spectral.shape[0]
     width_local = spectral.shape[1]
+    lat_half = lat_basis.shape[1]
     band_rows = cotangent.shape[0]
     block_cols = cotangent.shape[2]
     lon_total = block_cols * lax.axis_size("lon")
     first_row = lax.axis_index("lat") * pair_dev
     local_ids = lax.dynamic_slice_in_dim(pair_table, first_row, pair_dev)
     lower_part, upper_part, parity, first_len = pair_masks(local_ids, spectral.shape[2])
-    mirrored = jnp.flip(lat_basis * parity[:, None, :].astype(jnp.bfloat16), axis=1)
-    full_basis = jnp.concatenate([lat_basis, mirrored], axis=1)
-    lat_window = full_basis.shape[1]
-    masked = split_parts(spectral, lower_part, upper_part)
-    waves = jnp.einsum(
-        "pqkj,plj->pqlk", masked, full_basis, preferred_element_type=jnp.float32
+    rows = jnp.concatenate(
+        [lat_basis, lat_basis * parity[:, None, :].astype(jnp.bfloat16)], axis=1
+    )
+    zero = jnp.zeros_like(rows)
+    basis = jnp.stack(
+        [
+            jnp.where(lower_part[:, None, :], rows, zero),
+            jnp.where(upper_part[:, None, :], rows, zero),
+        ],
+        axis=1,
+    )
+    lat_window = 2 * lat_half
+    raw_waves = jnp.einsum(
+        "pqlj,pkj->pqlk", basis, spectral, preferred_element_type=jnp.float32
     ).astype(jnp.bfloat16)
+    waves = jnp.concatenate(
+        [raw_waves[:, :, :lat_half], jnp.flip(raw_waves[:, :, lat_half:], axis=2)], axis=2
+    )
     flat_waves = waves.reshape(2 * pair_dev, lat_window * width_local)
     band_waves = lax.all_to_all(flat_waves, "lat", split_axis=1, concat_axis=0, tiled=True)
     wave_count = band_waves.shape[0]
     coeff_grid = band_waves.reshape(wave_count, band_rows, width_local // 2, 2)
     numbers = wave_numbers(pair_table)
-    full_table = fourier_table(numbers, jnp.arange(lon_total, dtype=jnp.int32), lon_total)
+    full_table = fourier_table(numbers, lon_total)
     all_columns = jnp.einsum(
         "glkc,gcn->lkn", coeff_grid, full_table, preferred_element_type=jnp.float32
     ).astype(jnp.bfloat16)
@@ -81,7 +96,7 @@
         + out_bias[None, :, None]
     ).astype(jnp.bfloat16)
     out_weight_part = jnp.einsum(
-        "lch,lkc->hk", hidden, cotangent, preferred_element_type=jnp.float32
+        "lch,lkc->kh", hidden, cotangent, preferred_element_type=jnp.float32
     )
     out_bias_part = jnp.sum(cotangent.astype(jnp.float32), axis=(0, 2))
     hidden_grad = jnp.einsum(
@@ -93,9 +108,26 @@
     grid_grad = jnp.einsum(
         "lch,kh->lkc", pre_grad, in_weight, preferred_element_type=jnp.float32
     ).astype(jnp.bfloat16)
-    in_weight_grad, in_bias_grad, out_weight_grad, out_bias_grad = lax.psum(
-        (in_weight_part, in_bias_part, out_weight_part, out_bias_part), ("lat", "lon")
+    channels, hid = in_weight.shape
+    width = max(hid, channels)
+
+    def widen(v):
+        return jnp.pad(v, ((0, 0), (0, width - v.shape[1])))
+
+    stacked = jnp.concatenate(
+        [
+            widen(in_weight_part),
+            widen(out_weight_part),
+            widen(in_bias_part[None, :]),
+            widen(out_bias_part[None, :]),
+        ],
+        axis=0,
     )
+    summed = lax.psum(stacked, ("lat", "lon"))
+    in_weight_grad = summed[:channels, :hid]
+    out_weight_grad = summed[channels : 2 * channels, :hid].T
+    in_bias_grad = summed[2 * channels, :hid]
+    out_bias_grad = summed[2 * channels + 1, :channels]
     level_rows = lax.all_to_all(grid_grad, "lon", split_axis=1, concat_axis=2, tiled=True)
     wave_grad = jnp.einsum(
         "gcn,lkn->glkc", full_table, level_rows, preferred_element_type=jnp.float32
@@ -103,13 +135,11 @@
     flat_grad = wave_grad.reshape(wave_count, band_rows * width_local)
     pair_grad = lax.all_to_all(flat_grad, "lat", split_axis=0, concat_axis=1, tiled=True)
     pair_grad = pair_grad.reshape(pair_dev, 2, lat_window, width_local)
-    contrib = jnp.einsum(
-        "pqlk,plj->pqkj", pair_grad, full_basis, preferred_element_type=jnp.float32
+    pair_grad = jnp.concatenate(
+        [pair_grad[:, :, :lat_half], jnp.flip(pair_grad[:, :, lat_half:], axis=2)], axis=2
     )
-    empty = jnp.zeros_like(contrib[:, 0])
-    spectral_grad = (
-        jnp.where(lower_part[:, None, :], contrib[:, 0], empty)
-        + jnp.where(upper_part[:, None, :], contrib[:, 1], empty)
+    spectral_grad = jnp.einsum(
+        "pqlk,pqlj->pkj", pair_grad, basis, preferred_element_type=jnp.float32
     ).astype(jnp.bfloat16)
     return (tendency, spectral_grad, in_weight_grad, in_bias_grad, out_weight_grad, out_bias_grad)
 

time: 477 us -> 485 us (1.017)
  waiting for transfers between devices: 2.97 us -> 136 us
  other arithmetic: 128 us -> 59.6 us
  blocking collectives: 111 us -> 54.7 us
  matrix products: 108 us -> 85.8 us
  local copies, waits for them, and re-layouts: 91.9 us -> 113 us
    psum x1, waiting for transfers between devices: 2.94 us -> 136 us  [per_device(): summed = lax.psum(stacked, ('lat', 'lon'))]
    another operation x2 -> x1, other arithmetic: 81.6 us -> 13.9 us
    psum x1 -> x0, blocking collectives: 56.6 us -> none  [per_device(): lax.psum((in_weight_part, in_bias_part, out_weight_part, out_bias_part),...]
    convert_element_type x1 -> x0, other arithmetic: 36.2 us -> none  [per_device(): spectral_grad = (jnp.where(lower_part[:, None, :], contrib[:, 0], empty)...]
    dot_general x3, matrix products: 63.7 us -> 41.6 us  [the longest x1 20.5 us: per_device(): jnp.einsum('pqlk,pqlj->pkj', pair_grad, basis, preferred_element_type=jnp...]
    rev x1 -> x2, local copies, waits for them, and re-layouts: 20.3 us -> 6.02 us  [the longest x1 3.44 us: per_device(): jnp.flip(pair_grad[:, :, lat_half:], axis=2)]
    select_n x0 -> x1, other arithmetic: none -> 14.2 us  [per_device(): jnp.where(lower_part[:, None, :], rows, zero)]
    add x0 -> x1, local copies, waits for them, and re-layouts: none -> 14 us  [fourier_table(): sin_a[:, :, None] * cos_b[:, None, :]]
  transfers between devices with their start and end apart: 3 -> 3, of which waited for: 1 -> 1; matrix products, arithmetic and copies ran while one was open for 33% -> 17% of each run, Pallas kernels for 0% -> 0%
where the time goes in v1:
time: 485 us; the launch traced here: 477 us
  waiting for transfers between devices  136 us (28%)
  local copies, waits for them, and re-layouts  113 us (23%)
  matrix products  85.8 us (18%)
  other arithmetic  59.6 us (12%)
  blocking collectives  54.7 us (11%)
  between operations  14.6 us (3%)
  starting transfers between devices  13.7 us (3%)
    psum x1, waiting for transfers between devices, per_device(): summed = lax.psum(stacked, ('lat', 'lon'))  136 us
    all_to_all x1, blocking collectives, per_device(): lax.all_to_all(all_columns, 'lon', split_axis=2, concat_axis=1, tiled=True)  27.5 us
    all_to_all x1, blocking collectives, per_device(): lax.all_to_all(grid_grad, 'lon', split_axis=1, concat_axis=2, tiled=True)  27.2 us
    dot_general x1, matrix products, per_device(): jnp.einsum('pqlk,pqlj->pkj', pair_grad, basis, preferred_element_type=jnp...  20.5 us
    dot_general x1, matrix products, per_device(): jnp.einsum('pqlj,pkj->pqlk', basis, spectral, preferred_element_type=jnp....  20 us
    unnamed x30, local copies, waits for them, and re-layouts  17.3 us
    select_n x1, other arithmetic, per_device(): jnp.where(lower_part[:, None, :], rows, zero)  14.2 us
    add x1, local copies, waits for them, and re-layouts, fourier_table(): sin_a[:, :, None] * cos_b[:, None, :]  14 us
  transfers between devices with their start and end apart: 3, of which 1 were waited for; matrix products, arithmetic and copies ran while one was open for 17% of the time, Pallas kernels for 0%

profile of v1, /device:TPU:0, one launch (start us, length us, event | category | flops | bytes accessed | tf_op | source)
XLA Modules:
  0.0 477.3 jit_solution(11046358141665475062)
XLA Ops:
  8.6 7.1 %multiply_bitcast_fusion = bf16[80,1,32,1408]{3,2,1,0:T(8,128)(2,1)} fusion(bf16[80,32,1408]{2,1,0:T(8,128)(2,1)} %param.10, bf16[80,1408]{1,0:T(8,128)(2,1)S(1)} %select_convert_fusion), kind=kLoop, calls=%fused_computation.25 | loop fusion | flops 3604480 | bytes 14643200 | tf_op jit(solution)/shard_map/concatenate | solution.py:61
  15.7 14.2 %broadcast_select_fusion.1 = (bf16[80,1,64,1408]{3,2,1,0:T(8,128)(2,1)}, bf16[80,1,64,1408]{3,2,1,0:T(8,128)(2,1)}) fusion(pred[80,1408]{1,0:T(8,128)(4,1)S(1)} %get-tuple-element.22, bf16[80,1,32,1408]{3,2,1,0:T(8,128)(2,1)} %multiply_bitcast_fusion, bf16[80,1,32,1408]{3,2,1,0:T(8,128)(2,1)S(1)} %bitcast.97, pred[80,1408]{1,0:T(8,128)(4,1)S(1)} %get-tuple-element.23), kind=kLoop, calls=%fused_computation.8 | loop fusion | flops 43253760 | bytes 43479040 | tf_op jit(solution)/shard_map/jit(_where)/select_n | solution.py:67
  29.8 20.0 %fusion.18 = bf16[80,2,64,96]{3,2,1,0:T(8,128)(2,1)} fusion(bf16[80,96,1408]{2,1,0:T(8,128)(2,1)} %param.9, bf16[80,1,64,1408]{3,2,1,0:T(8,128)(2,1)} %get-tuple-element.7, bf16[80,1,64,1408]{3,2,1,0:T(8,128)(2,1)} %get-tuple-element.6), kind=kOutput, calls=%fused_computation.36 | convolution fusion | flops 2783641600 | bytes 52428800 | tf_op jit(solution)/shard_map/pqlj,pkj->pqlk/dot_general | solution.py:73
  64.6 7.5 %all-to-all-start = ((bf16[160,8,768]{2,0,1:T(8,128)(2,1)}), bf16[160,8,768]{2,0,1:T(8,128)(2,1)S(1)}, u32[]{:S(2)}, u32[]{:S(2)}) async-start(bf16[160,8,768]{2,0,1:T(8,128)(2,1)} %copy.25), calls=%async_computation | async-start | bytes 3932160 | tf_op jit(solution)/shard_map/all_to_all | solution.py:80
  76.5 13.6 %multiply_subtract_fusion = (f32[1280,20,128]{0,2,1:T(8,128)}, f32[1280,20,128]{0,2,1:T(8,128)}) fusion(f32[1280,128]{0,1:T(8,128)S(1)} %get-tuple-element.21, f32[1280,20]{0,1:T(8,128)} %get-tuple-element.17, f32[1280,128]{0,1:T(8,128)S(1)} %get-tuple-element.20, f32[1280,20]{0,1:T(8,128)} %get-tuple-element.16), kind=kLoop, calls=%fused_computation.13 | loop fusion | flops 19660800 | bytes 27729920 | tf_op jit(solution)/shard_map/sub | solution.py:39
  90.1 14.0 %copy.29 = f32[1280,1,2560]{2,0,1:T(8,128)} copy(f32[1280,1,2560]{0,2,1:T(8,128)} %bitcast.94) | data formatting | bytes 26214400 | tf_op jit(solution)/shard_map/add | solution.py:40
  104.1 14.0 %copy.28 = f32[1280,1,2560]{2,0,1:T(8,128)} copy(f32[1280,1,2560]{0,2,1:T(8,128)} %bitcast.93) | data formatting | bytes 26214400 | tf_op jit(solution)/shard_map/sub | solution.py:39
  118.1 13.9 %multiply_convert_fusion = (bf16[1280,1,2560]{2,0,1:T(8,128)(2,1)}, bf16[1280,1,2560]{2,0,1:T(8,128)(2,1)}) fusion(f32[1280,1,2560]{2,0,1:T(8,128)} %copy.29, f32[1280]{0:T(1024)S(1)} %get-tuple-element.19, f32[1280,1,2560]{2,0,1:T(8,128)} %copy.28, f32[1280]{0:T(1024)S(1)} %get-tuple-element.18), kind=kLoop, calls=%fused_computation.10 | loop fusion | flops 13107200 | bytes 39331840 | tf_op jit(solution)/shard_map/convert.1
  137.4 5.2 %reshape.454 = bf16[1280,8,48,2]{0,3,2,1:T(2,128)(2,1)} reshape(bf16[8,160,768]{1,0,2:T(8,128)(2,1)S(1)} %copy.26) | data formatting | bytes 3932160 | tf_op jit(solution)/shard_map/reshape | solution.py:82
  142.6 8.9 %fusion.12 = bf16[8,48,2560]{2,1,0:T(8,128)(2,1)S(1)} fusion(bf16[1280,1,2560]{2,0,1:T(8,128)(2,1)} %get-tuple-element.28, bf16[1280,1,2560]{2,0,1:T(8,128)(2,1)} %get-tuple-element.29, bf16[1280,8,48,2]{0,3,2,1:T(2,128)(2,1)} %reshape.454), kind=kOutput, calls=%fused_computation.27 | convolution fusion | flops 5040701440 | bytes 17039360 | tf_op jit(solution)/shard_map/glkc,gcn->lkn/dot_general | solution.py:85
  151.6 5.4 %copy.31 = bf16[8,48,2560]{1,0,2:T(8,128)(2,1)} copy(bf16[8,48,2560]{2,1,0:T(8,128)(2,1)S(1)} %fusion.12) | data formatting | bytes 3932160 | tf_op jit(solution)/shard_map/convert_element_type | solution.py:87
  157.0 8.8 %reshape.467 = bf16[4,2,122880]{2,1,0:T(2,128)(2,1)S(1)} reshape(bf16[2560,8,48]{2,1,0:T(8,128)(2,1)} %bitcast.98) | data formatting | bytes 3932160
  165.8 27.5 %all_to_all.68 = bf16[4,2,122880]{2,1,0:T(2,128)(2,1)} all-to-all(bf16[4,2,122880]{2,1,0:T(2,128)(2,1)S(1)} %reshape.467), channel_id=1, replica_groups=mesh['lat'=8,'lon'=4] {'lon'}, dimensions={0} | all-to-all | bytes 3932160 | tf_op jit(solution)/shard_map/all_to_all | solution.py:88
  193.4 7.1 %reshape.468 = bf16[2560,8,48]{2,1,0:T(8,128)(2,1)} reshape(bf16[4,2,122880]{2,1,0:T(2,128)(2,1)} %all_to_all.68) | data formatting | bytes 3932160
  200.4 5.7 %copy.32 = bf16[8,48,4,640]{3,1,2,0:T(8,128)(2,1)S(1)} copy(bf16[8,48,4,640]{1,0,3,2:T(8,128)(2,1)} %bitcast.99) | data formatting | bytes 3932160 | tf_op jit(solution)/shard_map/all_to_all | solution.py:88
  206.2 5.5 %multiply_convert_fusion.2 = (bf16[8,640,512]{2,1,0:T(8,128)(2,1)}, f32[8,640,512]{2,1,0:T(8,128)S(1)}) fusion(f32[512]{0:T(512)S(1)} %copy-done.8, bf16[8,192,640]{2,1,0:T(8,128)(2,1)S(1)} %bitcast.104, bf16[192,512]{1,0:T(8,128)(2,1)S(1)} %copy-done), kind=kOutput, calls=%fused_computation.22 | convolution fusion | flops 1032847360 | bytes 17893376 | tf_op jit(solution)/shard_map/lkc,kh->lch/dot_general | solution.py:90
  211.7 8.7 %convert_reduce_fusion = (f32[512]{0:T(512)S(1)}, bf16[8,640,512]{2,1,0:T(8,128)(2,1)S(1)}) fusion(f32[8,640,512]{2,1,0:T(8,128)S(1)} %get-tuple-element.25, f32[512]{0:T(512)S(1)} %copy-done.8, bf16[8,192,640]{2,1,0:T(8,128)(2,1)S(1)} %copy-done.3, bf16[512,192]{0,1:T(8,128)(2,1)S(1)} %copy-done.7), kind=kOutput, calls=%fused_computation.21 | convolution fusion | flops 1066925568 | bytes 17895424 | tf_op jit(solution)/shard_map/lkc,hk->lch/dot_general | solution.py:102
  223.4 27.2 %all_to_all.69 = bf16[8,192,640]{2,0,1:T(8,128)(2,1)S(1)} all-to-all(bf16[8,192,640]{2,0,1:T(8,128)(2,1)S(1)} %copy.33), channel_id=1, replica_groups=mesh['lat'=8,'lon'=4] {'lon'}, dimensions={1} | all-to-all | bytes 3932160 | tf_op jit(solution)/shard_map/all_to_all | solution.py:131
  254.3 9.0 %fusion.14 = bf16[1280,8,48,2]{0,2,3,1:T(8,128)(2,1)S(1)} fusion(bf16[1280,1,2560]{2,0,1:T(8,128)(2,1)} %get-tuple-element.28, bf16[1280,1,2560]{2,0,1:T(8,128)(2,1)} %get-tuple-element.29, bf16[8,48,2560,1]{2,1,0,3:T(8,128)(2,1)} %reshape.462), kind=kOutput, calls=%fused_computation.31 | convolution fusion | flops 5060362240 | bytes 17039360 | tf_op jit(solution)/shard_map/gcn,lkn->glkc/dot_general | solution.py:132
  266.0 6.4 %all_to_all.61 = bf16[8,160,768]{1,0,2:T(8,128)(2,1)S(1)} reshape(bf16[1280,8,48,2]{0,3,2,1:T(2,128)(2,1)} %copy.35) | data formatting | bytes 3932160 | tf_op jit(solution)/shard_map/all_to_all | solution.py:136
  275.7 6.0 %all-to-all-start.3 = ((bf16[8,160,768]{2,1,0:T(8,128)(2,1)}), bf16[8,160,768]{2,1,0:T(8,128)(2,1)S(1)}, u32[]{:S(2)}, u32[]{:S(2)}) async-start(bf16[8,160,768]{2,1,0:T(8,128)(2,1)} %copy.36), calls=%async_computation.3 | async-start | bytes 3932160 | tf_op jit(solution)/shard_map/all_to_all | solution.py:136
  290.9 5.6 %fusion.23 = bf16[8,192,640]{2,1,0:T(8,128)(2,1)} fusion(f32[192]{0:T(256)S(1)} %copy-done.9, bf16[8,640,512]{2,1,0:T(8,128)(2,1)} %get-tuple-element.24, bf16[512,192]{0,1:T(8,128)(2,1)S(1)} %copy-done.7), kind=kOutput, calls=%fused_computation.41 | convolution fusion | flops 1008599040 | bytes 7406336 | tf_op jit(solution)/shard_map/lch,hk->lkc/dot_general | solution.py:95
  296.5 136.0 %all-reduce.3.cloned.1.call-done = f32[386,512]{1,0:T(8,128)} async-done(((f32[386,512]{1,0:T(8,128)}), f32[386,512]{1,0:T(8,128)}) %all-reduce.3.cloned.1.call-update) | async-done | bytes 790544 | tf_op jit(solution)/shard_map/psum | solution.py:126
  449.8 20.5 %bitcast_convert_fusion = bf16[80,96,1408]{2,1,0:T(8,128)(2,1)} fusion(bf16[80,1,64,1408]{3,2,1,0:T(8,128)(2,1)} %get-tuple-element.7, bf16[80,1,64,1408]{3,2,1,0:T(8,128)(2,1)} %get-tuple-element.6, bf16[80,2,32,96]{3,2,1,0:T(8,128)(2,1)S(1)} %rev.8, bf16[80,2,32,96]{3,2,1,0:T(8,128)(2,1)} %get-tuple-element.8), kind=kOutput, calls=%fused_computation | convolution fusion | flops 2797404160 | bytes 52428800 | tf_op jit(solution)/shard_map/pqlk,pqlj->pkj/dot_general | solution.py:141
  (71 shorter events, 64.9 us)
Async XLA Ops:
  7.2 199.0 %copy-start = (bf16[192,512]{1,0:T(8,128)(2,1)S(1)}, bf16[192,512]{1,0:T(8,128)(2,1)}, u32[]{:S(2)}) copy-start(bf16[192,512]{1,0:T(8,128)(2,1)} %param.11) | copy-start | bytes 589828
  8.3 7.3 %slice-start = ((s8[7208960]{0:T(1024)(128)(4,1)}), s8[4194304]{0:T(1024)(128)(4,1)S(1)}, s32[]{:S(2)}) async-start(s8[7208960]{0:T(1024)(128)(4,1)} %bitcast.95), calls=%async_computation.5 | async-start | bytes 8388608
  8.6 7.1 %slice-start.1 = ((s8[7208960]{0:T(1024)(128)(4,1)}), s8[3014656]{0:T(1024)(128)(4,1)S(1)}, s32[]{:S(2)}) async-start(s8[7208960]{0:T(1024)(128)(4,1)} %bitcast.95), calls=%async_computation.6 | async-start | bytes 6029312
  58.3 13.9 %copy-start.6 = (s32[640]{0:T(1024)S(1)}, s32[640]{0:T(1024)}, u32[]{:S(2)}) copy-start(s32[640]{0:T(1024)} %param.8) | copy-start | bytes 7684
  64.6 67.4 %all-to-all-start = ((bf16[160,8,768]{2,0,1:T(8,128)(2,1)}), bf16[160,8,768]{2,0,1:T(8,128)(2,1)S(1)}, u32[]{:S(2)}, u32[]{:S(2)}) async-start(bf16[160,8,768]{2,0,1:T(8,128)(2,1)} %copy.25), calls=%async_computation | async-start | bytes 3932160 | tf_op jit(solution)/shard_map/all_to_all | solution.py:80
  132.0 1.3 copy-start.1
  193.4 12.8 %copy-start.8 = (f32[512]{0:T(512)S(1)}, f32[512]{0:T(512)}, u32[]{:S(2)}) copy-start(f32[512]{0:T(512)} %param.12) | copy-start | bytes 6148
  206.2 5.6 %copy-start.5 = (bf16[8,48,4,640]{3,1,2,0:T(8,128)(2,1)}, bf16[8,48,4,640]{3,1,2,0:T(8,128)(2,1)S(1)}, u32[]{:S(2)}) copy-start(bf16[8,48,4,640]{3,1,2,0:T(8,128)(2,1)S(1)} %copy.32) | copy-start | bytes 5898244
  206.2 5.5 %copy-start.3 = (bf16[8,192,640]{2,1,0:T(8,128)(2,1)S(1)}, bf16[8,192,640]{2,1,0:T(8,128)(2,1)}, u32[]{:S(2)}) copy-start(bf16[8,192,640]{2,1,0:T(8,128)(2,1)} %param.15) | copy-start | bytes 5898244
  206.2 5.5 %copy-start.7 = (bf16[512,192]{0,1:T(8,128)(2,1)S(1)}, bf16[512,192]{0,1:T(8,128)(2,1)}, u32[]{:S(2)}) copy-start(bf16[512,192]{0,1:T(8,128)(2,1)} %param.13) | copy-start | bytes 589828
  220.4 30.1 %copy-start.2 = (bf16[8,640,512]{2,1,0:T(8,128)(2,1)}, bf16[8,640,512]{2,1,0:T(8,128)(2,1)S(1)}, u32[]{:S(2)}) copy-start(bf16[8,640,512]{2,1,0:T(8,128)(2,1)S(1)} %get-tuple-element.27) | copy-start | bytes 15728644
  275.7 161.4 %all-to-all-start.3 = ((bf16[8,160,768]{2,1,0:T(8,128)(2,1)}), bf16[8,160,768]{2,1,0:T(8,128)(2,1)S(1)}, u32[]{:S(2)}, u32[]{:S(2)}) async-start(bf16[8,160,768]{2,1,0:T(8,128)(2,1)} %copy.36), calls=%async_computation.3 | async-start | bytes 3932160 | tf_op jit(solution)/shard_map/all_to_all | solution.py:136
  281.7 150.8 %all-reduce.3.cloned.1.call-start = ((), (), s32[]{:S(2)}) async-start(), calls=%async_computation.4 | async-start | bytes 1605632 | tf_op jit(solution)/shard_map/psum | solution.py:126
  281.9 6.7 %copy-start.4 = (bf16[8,192,640]{2,1,0:T(8,128)(2,1)S(1)}, bf16[8,192,640]{2,1,0:T(8,128)(2,1)}, u32[]{:S(2)}) copy-start(bf16[8,192,640]{2,1,0:T(8,128)(2,1)} %param.15) | copy-start | bytes 5898244
  281.9 6.7 %slice-start.2 = ((s8[5242880]{0:T(1024)(128)(4,1)}), s8[4194304]{0:T(1024)(128)(4,1)S(1)}, s32[]{:S(2)}) async-start(s8[5242880]{0:T(1024)(128)(4,1)} %bitcast.110), calls=%async_computation.7 | async-start | bytes 8388608
  284.0 4.6 slice-start.3
  288.6 2.3 copy-start.9
Sparse Core Ops, SparseCore 0:
  291.0 141.4 all-reduce.2
